TPU v7x, 32 devices: a whole 2x2x4 slice. The times are simulated.
32 devices in a mesh: grp: 2 (over x), wave: 16 (over z, y, core).
Axes of the slice: x: 2, y: 2, z: 4, core: 2. Of those that a mesh axis runs over, the one named last changes fastest.
Arguments:
- north_rows: bfloat16 [2560, 128, 274], P(('grp', 'wave')), parts along dimension 0, may hold values from -6 to 6
- south_rows: bfloat16 [2560, 128, 274], P(('grp', 'wave')), parts along dimension 0, may hold values from -6 to 6
- lon_counts: int32 [1280], replicated, may hold values from 20 to 5148, as said below
- slot_wave: int32 [128], replicated, may hold values from 0 to 2559, as said below
- legendre: bfloat16 [128, 1280, 1280], P('wave'), may hold values from -0.15625 to 0.15625
- mode_rates: float32 [137], replicated, may hold values from 0.05 to 20
- to_modes: bfloat16 [137, 137], replicated, may hold values from -0.5 to 0.5
- from_modes: bfloat16 [137, 137], replicated, may hold values from -0.5 to 0.5
Outputs:
- spec_state: bfloat16 [256, 1280, 274], P(('grp', 'wave')), parts along dimension 0
- new_rows: bfloat16 [2560, 128, 274], P(('grp', 'wave')), parts along dimension 0
There are 2 independent parts, one for each index of `grp`. A program takes and returns all parts, laid end to end along the dimension named above; an argument that names none is the same for every part. Nothing has to cross between parts.
Inputs may be any that keep to these rules, and one draw needn't show every extreme that they name: Wavenumber m is present in latitude row j only if 2 m is below lon_counts[j]. `slot_wave`: distinct zonal wavenumbers.
All inputs are finite; a program needn't handle non-finite values.
Results may differ from a plain program's by a relative error of at most 0.0065.
Values may be sent and summed in bfloat16 or wider, within the bound.
A program may use at most 192 MiB of HBM per device.

v0:
```python
import functools

import jax
import jax.numpy as jnp
from jax import lax
from jax.experimental import pallas as pl
from jax.experimental.pallas import tpu as pltpu
from jax.sharding import PartitionSpec as P

NMAX = 2559
VMEM_LIMIT = 60 * 1024 * 1024
STEP = 16
UNPACK_STEP = 24


def pack_kernel(own, counts_ref, waves_ref, north_ref, south_ref, out_ref, turned):
    lats = north_ref.shape[1]
    live = 2 * waves_ref[...] < counts_ref[...]
    total = north_ref[...].astype(jnp.float32) + south_ref[...].astype(jnp.float32)
    kept = jnp.where(live[None], total, 0.0).astype(jnp.bfloat16)
    turned[...] = jnp.swapaxes(kept, 1, 2).astype(jnp.float32)
    for d in range(out_ref.shape[0]):
        for i in range(own):
            rows = turned[:, own * d + i, :].astype(jnp.bfloat16)
            out_ref[d, :, lats * i : lats * (i + 1)] = rows


def pack(part, own, first, levels, north, south, counts, waves):
    _, lats, slots = north.shape
    start = first // STEP
    rows = pl.BlockSpec((STEP, lats, slots), lambda g: (start + g, 0, 0))
    return pl.pallas_call(
        functools.partial(pack_kernel, own),
        grid=(pl.cdiv(levels, STEP),),
        in_specs=[
            pl.BlockSpec((lats, 1), lambda g: (0, 0)),
            pl.BlockSpec((1, slots), lambda g: (0, 0)),
            rows,
            rows,
        ],
        out_specs=pl.BlockSpec((slots // own, STEP, own * lats), lambda g: (0, g, 0)),
        out_shape=jax.ShapeDtypeStruct((slots // own, levels, own * lats), jnp.bfloat16),
        scratch_shapes=[pltpu.VMEM((STEP, slots, lats), jnp.float32)],
        cost_estimate=pl.CostEstimate(flops=0, bytes_accessed=levels * lats * slots * 6, transcendentals=0),
        name=f"pack{part}",
    )(counts, waves, north, south)


def unpack_kernel(own, in_ref, *refs):
    out_ref, turned = refs[-2:]
    lats = out_ref.shape[2]
    for d in range(in_ref.shape[0]):
        for i in range(own):
            rows = in_ref[d, :, lats * i : lats * (i + 1)]
            turned[own * d + i] = rows.astype(jnp.float32)
    for c in range(out_ref.shape[1]):
        out_ref[0, c] = turned[:, c, :].T.astype(jnp.bfloat16)


def unpack(part, own, packed, placed):
    senders, levels, width = packed.shape
    lats, slots = width // own, senders * own
    in_specs = [pl.BlockSpec((senders, UNPACK_STEP, width), lambda g: (0, g, 0))]
    operands = [packed]
    aliases = {}
    if placed is not None:
        in_specs.append(pl.BlockSpec(memory_space=pl.ANY))
        operands.append(placed)
        aliases = {1: 0}
    return pl.pallas_call(
        functools.partial(unpack_kernel, own),
        grid=(pl.cdiv(levels, UNPACK_STEP),),
        in_specs=in_specs,
        out_specs=pl.BlockSpec((1, UNPACK_STEP, lats, slots), lambda g: (part, g, 0, 0)),
        out_shape=jax.ShapeDtypeStruct((2, levels, lats, slots), jnp.bfloat16),
        scratch_shapes=[pltpu.VMEM((slots, UNPACK_STEP, lats), jnp.float32)],
        input_output_aliases=aliases,
        cost_estimate=pl.CostEstimate(flops=0, bytes_accessed=levels * lats * slots * 4, transcendentals=0),
        name=f"unpack{part}",
    )(*operands)


def compute_kernel(
    own, senders, lats, takes, waves_ref, counts_ref, rates_ref, to_ref, from_ref, leg_ref,
    *refs,
):
    *pieces, state_ref, back_ref, columns, returned = refs
    slot = pl.program_id(0)

    @pl.when(slot == 0)
    def _():
        for s in range(own):
            for d in range(senders):
                lanes = slice(lats * d, lats * (d + 1))
                done = 0
                for (skip, count), rows_ref in zip(takes, pieces):
                    piece = rows_ref[d, skip : skip + count, lats * s : lats * (s + 1)]
                    columns[s, done : done + count, lanes] = piece
                    done += count

    wave = waves_ref[slot]
    direct = lax.dot_general(
        columns[slot], leg_ref[0], (((1,), (1,)), ((), ())), preferred_element_type=jnp.float32
    ).astype(jnp.bfloat16)
    modal = jnp.dot(to_ref[...], direct, preferred_element_type=jnp.float32)
    degree = wave + 2 * lax.broadcasted_iota(jnp.int32, (1, leg_ref.shape[1]), 1)
    degree_f = degree.astype(jnp.float32)
    scaled_degree = degree_f * (degree_f + 1.0) / float(NMAX * (NMAX + 1))
    divisor = 1.0 + rates_ref[...] * scaled_degree
    scaled = (modal / divisor).astype(jnp.bfloat16)
    state = jnp.dot(from_ref[...], scaled, preferred_element_type=jnp.float32)
    state = jnp.where(degree <= NMAX, state, 0.0).astype(jnp.bfloat16)
    state_ref[0] = state
    back = jnp.dot(state, leg_ref[0], preferred_element_type=jnp.float32)
    returned[slot] = jnp.where(2 * wave < counts_ref[...], back, 0.0).astype(jnp.bfloat16)

    @pl.when(slot == own - 1)
    def _():
        for s in range(own):
            for d in range(senders):
                back_ref[d, :, lats * s : lats * (s + 1)] = returned[s, :, lats * d : lats * (d + 1)]


def compute(rows, takes, legendre, own_waves, counts, rates, to_t, from_t):
    senders, _, width = rows[0].shape
    levels = to_t.shape[0]
    own, row_total, lat_total = legendre.shape
    lats = lat_total // senders
    whole = lambda *shape: pl.BlockSpec(shape, lambda s, w: (0,) * len(shape))
    return pl.pallas_call(
        functools.partial(compute_kernel, own, senders, lats, takes),
        grid_spec=pltpu.PrefetchScalarGridSpec(
            num_scalar_prefetch=1,
            grid=(own,),
            in_specs=[
                whole(1, lat_total),
                whole(levels, 1),
                whole(levels, levels),
                whole(levels, levels),
                pl.BlockSpec((1, row_total, lat_total), lambda s, w: (s, 0, 0)),
                *[whole(*piece.shape) for piece in rows],
            ],
            out_specs=[
                pl.BlockSpec((1, levels, row_total), lambda s, w: (s, 0, 0)),
                whole(senders, levels, width),
            ],
            scratch_shapes=[
                pltpu.VMEM((own, levels, lat_total), jnp.bfloat16),
                pltpu.VMEM((own, levels, lat_total), jnp.bfloat16),
            ],
        ),
        out_shape=[
            jax.ShapeDtypeStruct((own, levels, row_total), jnp.bfloat16),
            jax.ShapeDtypeStruct((senders, levels, width), jnp.bfloat16),
        ],
        compiler_params=pltpu.CompilerParams(vmem_limit_bytes=VMEM_LIMIT),
        cost_estimate=pl.CostEstimate(
            flops=8 * own * row_total * lat_total * levels,
            bytes_accessed=2 * own * row_total * lat_total,
            transcendentals=0,
        ),
        name="legendre",
    )(own_waves, counts, rates, to_t, from_t, legendre, *rows)


def per_device(
    north_rows, south_rows, lon_counts, slot_wave, legendre, mode_rates, to_modes, from_modes
):
    lat_dev = north_rows.shape[0]
    slot_dev, row_total, lat_total = legendre.shape
    levels = to_modes.shape[0]
    my_index = lax.axis_index("wave")
    own_waves = lax.dynamic_slice_in_dim(slot_wave, my_index * slot_dev, slot_dev)
    local_counts = lax.dynamic_slice_in_dim(lon_counts, my_index * lat_dev, lat_dev)
    slots = slot_wave.shape[0]
    north = jnp.transpose(north_rows, (2, 0, 1))
    south = jnp.transpose(south_rows, (2, 0, 1))
    counts_here, waves_all = local_counts[:, None], slot_wave[None, :]
    counts_all, rates = lon_counts[None, :], mode_rates[:, None]
    to_t, from_t = to_modes.T, from_modes.T
    head = pl.cdiv(levels, STEP) * STEP
    moved, states, placed = [], [], None
    for part, (first, count) in enumerate(((0, head), (head, 2 * levels - head))):
        packed = pack(part, slot_dev, first, count, north, south, counts_here, waves_all)
        moved.append(lax.all_to_all(packed, "wave", split_axis=0, concat_axis=0, tiled=True))
    cuts = (
        (moved[:1], ((0, levels),)),
        (moved, ((levels, head - levels), (0, 2 * levels - head))),
    )
    for part, (rows, takes) in enumerate(cuts):
        state, back = compute(
            rows, takes, legendre, own_waves, counts_all, rates, to_t, from_t
        )
        home = lax.all_to_all(back, "wave", split_axis=0, concat_axis=0, tiled=True)
        states.append(jnp.transpose(state, (1, 0, 2)))
        placed = unpack(part, slot_dev, home, placed)
    spec_state = jnp.transpose(jnp.concatenate(states, axis=0), (1, 2, 0))
    new_rows = jnp.transpose(placed.reshape(2 * levels, lat_dev, slots), (1, 2, 0))
    return (spec_state, new_rows)


def solution(mesh):
    in_specs = (
        P(("grp", "wave"), None, None),
        P(("grp", "wave"), None, None),
        P(),
        P(),
        P("wave", None, None),
        P(),
        P(),
        P(),
    )
    out_specs = (P(("grp", "wave"), None, None), P(("grp", "wave"), None, None))
    return jax.shard_map(
        per_device, mesh=mesh, in_specs=in_specs, out_specs=out_specs, check_vma=False
    )
```

profile of v0, /device:TPU:13, one launch (start us, length us, event | category | flops | bytes accessed | tf_op | source)
XLA Modules:
  0.0 305.4 jit_solution(8370832150827818945)
XLA Ops:
  0.6 0.8 dynamic-slice_bitcast_fusion
  1.4 0.7 copy.18.counts_ref
  2.1 14.0 %pack0.1 = bf16[16,144,640]{2,1,0:T(8,128)(2,1)} custom-call(s32[80,1]{1,0:T(8,128)} %copy.18.counts_ref, s32[1,128]{1,0:T(1,128)} %bitcast.26, bf16[274,80,128]{2,1,0:T(8,128)(2,1)} %bitcast.15, bf16[274,80,128]{2,1,0:T(8,128)(2,1)} %bitcast.17), custom_call_target="tpu_custom_call" | custom-call | bytes 8847360 | tf_op jit(solution)/shard_map/pack0/pallas_call | solution.py:32
  16.2 6.5 %all-to-all-start = ((bf16[16,144,640]{2,1,0:T(8,128)(2,1)}), bf16[16,144,640]{2,1,0:T(8,128)(2,1)S(1)}, u32[]{:S(2)}, u32[]{:S(2)}) async-start(bf16[16,144,640]{2,1,0:T(8,128)(2,1)} %pack0.1), calls=%async_computation | async-start | bytes 5898240 | tf_op jit(solution)/shard_map/all_to_all | solution.py:185
  22.7 0.0 copy-start.4
  22.7 0.0 copy-start.5
  22.7 0.0 copy-start.6
  22.7 14.1 %pack1.1 = bf16[16,130,640]{2,1,0:T(8,128)(2,1)} custom-call(s32[80,1]{1,0:T(8,128)} %copy.18.counts_ref, s32[1,128]{1,0:T(1,128)} %bitcast.27, bf16[274,80,128]{2,1,0:T(8,128)(2,1)} %bitcast.16, bf16[274,80,128]{2,1,0:T(8,128)(2,1)} %bitcast.18), custom_call_target="tpu_custom_call" | custom-call | bytes 7987200 | tf_op jit(solution)/shard_map/pack1/pallas_call | solution.py:32
  36.8 0.0 copy-start.2
  36.8 0.0 copy-start.3
  36.8 51.5 %all-to-all-done.refs_0_ = bf16[16,144,640]{2,1,0:T(8,128)(2,1)S(1)} async-done(((bf16[16,144,640]{2,1,0:T(8,128)(2,1)}), bf16[16,144,640]{2,1,0:T(8,128)(2,1)S(1)}, u32[]{:S(2)}, u32[]{:S(2)}) %all-to-all-start) | async-done | bytes 2949152 | tf_op jit(solution)/shard_map/all_to_all | solution.py:185
  88.4 0.0 copy-start.1
  88.4 4.8 %all-to-all-start.1 = ((bf16[16,130,640]{2,1,0:T(8,128)(2,1)}), bf16[16,130,640]{2,1,0:T(8,128)(2,1)}, u32[]{:S(2)}, u32[]{:S(2)}) async-start(bf16[16,130,640]{2,1,0:T(8,128)(2,1)} %pack1.1), calls=%async_computation.1 | async-start | bytes 5570560 | tf_op jit(solution)/shard_map/all_to_all | solution.py:185
  93.1 0.0 copy-done.4
  93.1 0.6 broadcast_in_dim.12.counts_ref
  93.7 0.0 copy-done.5
  93.7 0.6 dynamic_slice.6.waves_ref
  94.4 0.0 copy-done.6
  94.4 0.8 copy.19.rates_ref
  95.1 0.0 copy-done.2
  95.2 0.7 copy.16
  95.9 0.0 copy-done.3
  95.9 0.7 copy.17
  96.6 0.0 copy-done.1
  96.6 28.5 %legendre.2 = (bf16[8,137,1280]{2,1,0:T(8,128)(2,1)}, bf16[16,137,640]{2,1,0:T(8,128)(2,1)}) custom-call(s32[8]{0:T(128)} %dynamic_slice.6.waves_ref, s32[1,1280]{1,0:T(1,128)} %broadcast_in_dim.12.counts_ref, f32[137,1]{1,0:T(8,128)} %copy.19.rates_ref, bf16[137,137]{1,0:T(8,128)(2,1)} %bitcast.22, bf16[137,137]{1,0:T(8,128)(2,1)} %bitcast.24, ...), custom_call_target="tpu_custom_call" | custom-call | flops 14365491200 | bytes 26214400 | tf_op jit(solution)/shard_map/legendre/pallas_call | solution.py:130
  125.1 30.3 %all-to-all-done.1.refs_1_ = bf16[16,130,640]{2,1,0:T(8,128)(2,1)} async-done(((bf16[16,130,640]{2,1,0:T(8,128)(2,1)}), bf16[16,130,640]{2,1,0:T(8,128)(2,1)}, u32[]{:S(2)}, u32[]{:S(2)}) %all-to-all-start.1) | async-done | bytes 2662432 | tf_op jit(solution)/shard_map/all_to_all | solution.py:185
  155.4 4.8 %all-to-all-start.3 = ((bf16[16,137,640]{2,1,0:T(8,128)(2,1)}), bf16[16,137,640]{2,1,0:T(8,128)(2,1)S(1)}, u32[]{:S(2)}, u32[]{:S(2)}) async-start(bf16[16,137,640]{2,1,0:T(8,128)(2,1)} %get-tuple-element.9), calls=%async_computation.3 | async-start | bytes 5898240 | tf_op jit(solution)/shard_map/all_to_all | solution.py:194
  160.2 30.2 %legendre.3 = (bf16[8,137,1280]{2,1,0:T(8,128)(2,1)}, bf16[16,137,640]{2,1,0:T(8,128)(2,1)}) custom-call(s32[8]{0:T(128)} %dynamic_slice.6.waves_ref, s32[1,1280]{1,0:T(1,128)} %broadcast_in_dim.12.counts_ref, f32[137,1]{1,0:T(8,128)} %copy.19.rates_ref, bf16[137,137]{1,0:T(8,128)(2,1)} %bitcast.23, bf16[137,137]{1,0:T(8,128)(2,1)} %bitcast.25, ...), custom_call_target="tpu_custom_call" | custom-call | flops 14365491200 | bytes 26214400 | tf_op jit(solution)/shard_map/legendre/pallas_call | solution.py:130
  190.3 35.5 %all-to-all-done.3.in_ref = bf16[16,137,640]{2,1,0:T(8,128)(2,1)S(1)} async-done(((bf16[16,137,640]{2,1,0:T(8,128)(2,1)}), bf16[16,137,640]{2,1,0:T(8,128)(2,1)S(1)}, u32[]{:S(2)}, u32[]{:S(2)}) %all-to-all-start.3) | async-done | bytes 2805792 | tf_op jit(solution)/shard_map/all_to_all | solution.py:194
  225.9 0.0 copy-start
  225.9 4.8 %all-to-all-start.2 = ((bf16[16,137,640]{2,1,0:T(8,128)(2,1)}), bf16[16,137,640]{2,1,0:T(8,128)(2,1)}, u32[]{:S(2)}, u32[]{:S(2)}) async-start(bf16[16,137,640]{2,1,0:T(8,128)(2,1)} %get-tuple-element.8), calls=%async_computation.2 | async-start | bytes 5898240 | tf_op jit(solution)/shard_map/all_to_all | solution.py:194
  230.6 3.5 %maximum_bitcast_fusion = bf16[8,1280,274]{1,2,0:T(8,128)(2,1)S(1)} fusion(bf16[137,8,1280]{2,0,1:T(8,128)(2,1)} %bitcast.21, bf16[137,8,1280]{2,0,1:T(8,128)(2,1)} %bitcast.20), kind=kLoop, calls=%fused_computation | loop fusion | flops 11223040 | bytes 11223040 | tf_op jit(solution)/shard_map/transpose | solution.py:197
  234.2 0.0 copy-done
  234.2 3.6 %copy.22 = bf16[8,1280,274]{1,0,2:T(8,128)(2,1)} copy(bf16[8,1280,274]{1,2,0:T(8,128)(2,1)S(1)} %maximum_bitcast_fusion) | data formatting | bytes 11223040
  237.7 8.9 %unpack0.1.refs_0_ = bf16[2,137,80,128]{3,2,1,0:T(8,128)(2,1)} custom-call(bf16[16,137,640]{2,1,0:T(8,128)(2,1)} %copy-done), custom_call_target="tpu_custom_call" | custom-call | bytes 5611520 | tf_op jit(solution)/shard_map/unpack0/pallas_call | solution.py:70
  246.7 49.8 %all-to-all-done.2.in_ref = bf16[16,137,640]{2,1,0:T(8,128)(2,1)} async-done(((bf16[16,137,640]{2,1,0:T(8,128)(2,1)}), bf16[16,137,640]{2,1,0:T(8,128)(2,1)}, u32[]{:S(2)}, u32[]{:S(2)}) %all-to-all-start.2) | async-done | bytes 2805792 | tf_op jit(solution)/shard_map/all_to_all | solution.py:194
  296.4 8.9 %unpack1.1 = bf16[2,137,80,128]{3,2,1,0:T(8,128)(2,1)} custom-call(bf16[16,137,640]{2,1,0:T(8,128)(2,1)} %all-to-all-done.2.in_ref, bf16[2,137,80,128]{3,2,1,0:T(8,128)(2,1)} %unpack0.1.refs_0_), custom_call_target="tpu_custom_call", output_to_operand_aliasing={{}: (1, {})} | custom-call | bytes 5611520 | tf_op jit(solution)/shard_map/unpack1/pallas_call | solution.py:70
Async XLA Ops:
  16.2 72.2 %all-to-all-start = ((bf16[16,144,640]{2,1,0:T(8,128)(2,1)}), bf16[16,144,640]{2,1,0:T(8,128)(2,1)S(1)}, u32[]{:S(2)}, u32[]{:S(2)}) async-start(bf16[16,144,640]{2,1,0:T(8,128)(2,1)} %pack0.1), calls=%async_computation | async-start | bytes 5898240 | tf_op jit(solution)/shard_map/all_to_all | solution.py:185
  22.7 70.5 %copy-start.4 = (s32[1280]{0:T(1024)S(1)}, s32[1280]{0:T(1024)}, u32[]{:S(2)}) copy-start(s32[1280]{0:T(1024)} %param.10) | copy-start | bytes 15364
  22.7 71.1 %copy-start.5 = (s32[128]{0:T(128)S(1)}, s32[128]{0:T(128)}, u32[]{:S(2)}) copy-start(s32[128]{0:T(128)} %param.11) | copy-start | bytes 1540
  22.7 71.7 %copy-start.6 = (f32[137]{0:T(256)S(1)}, f32[137]{0:T(256)}, u32[]{:S(2)}) copy-start(f32[137]{0:T(256)} %param.13) | copy-start | bytes 1648
  36.8 58.3 %copy-start.2 = (bf16[137,137]{1,0:T(8,128)(2,1)S(1)}, bf16[137,137]{1,0:T(8,128)(2,1)}, u32[]{:S(2)}) copy-start(bf16[137,137]{1,0:T(8,128)(2,1)} %param.14) | copy-start | bytes 112618
  36.8 59.0 %copy-start.3 = (bf16[137,137]{1,0:T(8,128)(2,1)S(1)}, bf16[137,137]{1,0:T(8,128)(2,1)}, u32[]{:S(2)}) copy-start(bf16[137,137]{1,0:T(8,128)(2,1)} %param.15) | copy-start | bytes 112618
  88.4 8.3 %copy-start.1 = (bf16[16,144,640]{2,1,0:T(8,128)(2,1)}, bf16[16,144,640]{2,1,0:T(8,128)(2,1)S(1)}, u32[]{:S(2)}) copy-start(bf16[16,144,640]{2,1,0:T(8,128)(2,1)S(1)} %all-to-all-done.refs_0_) | copy-start | bytes 8847364
  88.4 67.0 %all-to-all-start.1 = ((bf16[16,130,640]{2,1,0:T(8,128)(2,1)}), bf16[16,130,640]{2,1,0:T(8,128)(2,1)}, u32[]{:S(2)}, u32[]{:S(2)}) async-start(bf16[16,130,640]{2,1,0:T(8,128)(2,1)} %pack1.1), calls=%async_computation.1 | async-start | bytes 5570560 | tf_op jit(solution)/shard_map/all_to_all | solution.py:185
  155.4 70.5 %all-to-all-start.3 = ((bf16[16,137,640]{2,1,0:T(8,128)(2,1)}), bf16[16,137,640]{2,1,0:T(8,128)(2,1)S(1)}, u32[]{:S(2)}, u32[]{:S(2)}) async-start(bf16[16,137,640]{2,1,0:T(8,128)(2,1)} %get-tuple-element.9), calls=%async_computation.3 | async-start | bytes 5898240 | tf_op jit(solution)/shard_map/all_to_all | solution.py:194
  225.9 8.3 %copy-start = (bf16[16,137,640]{2,1,0:T(8,128)(2,1)}, bf16[16,137,640]{2,1,0:T(8,128)(2,1)S(1)}, u32[]{:S(2)}) copy-start(bf16[16,137,640]{2,1,0:T(8,128)(2,1)S(1)} %all-to-all-done.3.in_ref) | copy-start | bytes 8417284
  225.9 70.6 %all-to-all-start.2 = ((bf16[16,137,640]{2,1,0:T(8,128)(2,1)}), bf16[16,137,640]{2,1,0:T(8,128)(2,1)}, u32[]{:S(2)}, u32[]{:S(2)}) async-start(bf16[16,137,640]{2,1,0:T(8,128)(2,1)} %get-tuple-element.8), calls=%async_computation.2 | async-start | bytes 5898240 | tf_op jit(solution)/shard_map/all_to_all | solution.py:194
where the time goes:
time: 306 us; the launch traced here: 305 us
  waiting for transfers between devices  167 us (55%)
  Pallas kernels  105 us (34%)
  starting transfers between devices  20.8 us (7%)
  local copies, waits for them, and re-layouts  8.52 us (3%)
  other arithmetic  3.53 us (1%)
    all_to_all x2, waiting for transfers between devices, per_device(): home = lax.all_to_all(back, 'wave', split_axis=0, concat_axis=0, tiled=True)  85.3 us
    all_to_all x2, waiting for transfers between devices, per_device(): lax.all_to_all(packed, 'wave', split_axis=0, concat_axis=0, tiled=True)  81.9 us
    pallas_call x2, Pallas kernels, compute(): pl.pallas_call(functools.partial(compute_kernel, own, senders, lats, take...  58.6 us
    pallas_call x2, Pallas kernels, pack(): pl.pallas_call(functools.partial(pack_kernel, own), grid=(pl.cdiv(levels,...  28.2 us
    pallas_call x2, Pallas kernels, unpack(): pl.pallas_call(functools.partial(unpack_kernel, own), grid=(pl.cdiv(level...  17.9 us
    all_to_all x2, starting transfers between devices, per_device(): lax.all_to_all(packed, 'wave', split_axis=0, concat_axis=0, tiled=True)  11.3 us
    all_to_all x2, starting transfers between devices, per_device(): home = lax.all_to_all(back, 'wave', split_axis=0, concat_axis=0, tiled=True)  9.56 us
  transfers between devices with their start and end apart: 4, of which 4 were waited for; matrix products, arithmetic and copies ran while one was open for 3% of the time, Pallas kernels for 27%

commit v1 on v0

v1 whole, which is shorter than its diff:
```python
import functools

import jax
import jax.numpy as jnp
from jax import lax
from jax.experimental import pallas as pl
from jax.experimental.pallas import tpu as pltpu
from jax.sharding import PartitionSpec as P

NMAX = 2559
VMEM_LIMIT = 63 * 1024 * 1024
STEP = 16
MESH = pl.DeviceIdType.MESH


def align(rows):
    return pl.cdiv(rows, STEP) * STEP


def back_cuts(levels):
    total = 2 * levels
    ready = levels // STEP * STEP
    half = ready // 2 // STEP * STEP
    cuts = [0, half, ready]
    rest = total // STEP - ready // STEP
    for part in (1, 2):
        cuts.append(ready + rest * part // 3 * STEP)
    cuts.append(total // STEP * STEP - STEP)
    cuts.append(total)
    return tuple(zip(cuts[:-1], cuts[1:]))


def step_kernel(
    n, own, lats, levels,
    waves_s, counts_s, waves_ref, rates_ref, to_ref, from_ref, north, south, leg,
    spec_out, rows_out,
    inbuf, live, turned, sendbuf, recv, columns, returned, legbuf, to_t, from_t, rates_col,
    state_t, state_b, backbuf, backrecv, turned_back, outbuf,
    in_sem, leg_sem, send_sem, recv_sem, back_send_sem, back_recv_sem, state_sem, out_sem,
):
    me = lax.axis_index("wave")
    total = 2 * levels
    full = total // STEP
    tail = total - full * STEP
    split = align(levels)
    steps_a = split // STEP
    cuts = back_cuts(levels)

    barrier = pltpu.get_barrier_semaphore()

    def greet(r, carry):
        peer = lax.rem(me + r, n)
        pl.semaphore_signal(barrier, inc=1, device_id={"wave": peer}, device_id_type=MESH)
        return carry

    lax.fori_loop(1, n, greet, 0)

    def fetch(first, count, slot):
        return [
            pltpu.make_async_copy(
                src.at[pl.ds(first, count)],
                inbuf.at[slot, i, pl.ds(0, count)],
                in_sem.at[slot, i],
            )
            for i, src in enumerate((north, south))
        ]

    def fetch_leg(slot, place):
        return pltpu.make_async_copy(leg.at[slot], legbuf.at[place], leg_sem.at[place])

    for slot in range(2):
        for copy in fetch(slot * STEP, STEP, slot):
            copy.start()

    def fill(j, carry):
        count = counts_s[me * lats + j]
        live[pl.ds(j, 1), :] = jnp.where(2 * waves_ref[...] < count, 1.0, 0.0)
        return carry

    lax.fori_loop(0, lats, fill, 0)

    def send(src, dst, first, count, ssem, rsem):
        rows = pl.ds(first, count)

        def one(r, carry):
            peer = lax.rem(me + r, n)
            pltpu.make_async_remote_copy(
                src_ref=src.at[peer, rows],
                dst_ref=dst.at[me, rows],
                send_sem=ssem,
                recv_sem=rsem,
                device_id={"wave": peer},
                device_id_type=MESH,
            ).start()
            return carry

        lax.fori_loop(1, n, one, 0)
        pltpu.make_async_copy(src.at[me, rows], dst.at[me, rows], rsem).start()

    def pack(first, count, slot):
        sums = inbuf[slot, 0, :count].astype(jnp.float32) + inbuf[slot, 1, :count].astype(jnp.float32)
        kept = jnp.where(live[...][None] > 0.5, sums, 0.0).astype(jnp.bfloat16)
        turned[:count] = jnp.swapaxes(kept, 1, 2).astype(jnp.float32)
        for d in range(n):
            for i in range(own):
                rows = turned[:count, own * d + i, :].astype(jnp.bfloat16)
                sendbuf[d, pl.ds(first, count), lats * i : lats * (i + 1)] = rows

    def pack_step(g, carry):
        slot = lax.rem(g, 2)
        for copy in fetch(g * STEP, STEP, slot):
            copy.wait()
        pack(pl.multiple_of(g * STEP, STEP), STEP, slot)

        @pl.when(g + 2 < full)
        def _():
            for copy in fetch((g + 2) * STEP, STEP, slot):
                copy.start()

        @pl.when(g == 0)
        def _():
            pl.semaphore_wait(barrier, n - 1)

        @pl.when(g > 0)
        def _():
            part = (g - 1) // steps_a
            send(
                sendbuf, recv, pl.multiple_of((g - 1) * STEP, STEP), STEP,
                send_sem, recv_sem.at[part],
            )

        return carry

    lax.fori_loop(0, full, pack_step, 0)
    last = full * STEP - STEP
    if tail:
        for copy in fetch(full * STEP, tail, 0):
            copy.start()
        for copy in fetch(full * STEP, tail, 0):
            copy.wait()
        pack(full * STEP, tail, 0)
    for slot in range(2):
        fetch_leg(slot, slot).start()
    to_t[...] = to_ref[...].astype(jnp.float32).T.astype(jnp.bfloat16)
    from_t[...] = from_ref[...].astype(jnp.float32).T.astype(jnp.bfloat16)
    across = lax.broadcasted_iota(jnp.int32, (levels, levels), 1)
    down = lax.broadcasted_iota(jnp.int32, (levels, levels), 0)
    spread = jnp.where(across == down, jnp.broadcast_to(rates_ref[...], (levels, levels)), 0.0)
    rates_col[...] = jnp.sum(spread, axis=1, keepdims=True)
    send(sendbuf, recv, last, STEP + tail, send_sem, recv_sem.at[1])

    for part in range(2):
        arrived = recv.at[:, pl.ds(split * part, (split, total - split)[part])]
        pltpu.make_async_copy(arrived, arrived, recv_sem.at[part]).wait()
        base = levels * part
        for s in range(own):
            for d in range(n):
                piece = recv[d, base : base + levels, lats * s : lats * (s + 1)]
                columns[s, :, lats * d : lats * (d + 1)] = piece

        def solve(slot, carry):
            place = lax.rem(slot + own * part, 2)
            fetch_leg(slot, place).wait()
            wave = waves_s[me * own + slot]
            direct = lax.dot_general(
                columns[slot], legbuf[place], (((1,), (1,)), ((), ())),
                preferred_element_type=jnp.float32,
            ).astype(jnp.bfloat16)
            modal = jnp.dot(to_t[...], direct, preferred_element_type=jnp.float32)
            degree = wave + 2 * lax.broadcasted_iota(jnp.int32, (1, legbuf.shape[1]), 1)
            degree_f = degree.astype(jnp.float32)
            scaled_degree = degree_f * (degree_f + 1.0) / float(NMAX * (NMAX + 1))
            divisor = 1.0 + rates_col[...] * scaled_degree
            scaled = (modal / divisor).astype(jnp.bfloat16)
            state = jnp.dot(from_t[...], scaled, preferred_element_type=jnp.float32)
            state = jnp.where(degree <= NMAX, state, 0.0).astype(jnp.bfloat16)
            state_t[:, slot, :] = state.astype(jnp.float32)
            back = jnp.dot(state, legbuf[place], preferred_element_type=jnp.float32)
            returned[slot] = back.astype(jnp.bfloat16)
            later = slot + 2

            @pl.when(own * part + later < 2 * own)
            def _():
                fetch_leg(lax.rem(later, own), place).start()

            return carry

        lax.fori_loop(0, own, solve, 0)
        for s in range(own):
            for d in range(n):
                backbuf[d, base : base + levels, lats * s : lats * (s + 1)] = returned[
                    s, :, lats * d : lats * (d + 1)
                ]
        placed = pltpu.make_async_copy(state_b, spec_out.at[pl.ds(base, levels)], state_sem)
        if part == 1:
            pltpu.make_async_copy(state_b, spec_out.at[pl.ds(0, levels)], state_sem).wait()

        def narrow(l, carry):
            state_b[l] = state_t[l].astype(jnp.bfloat16)
            return carry

        lax.fori_loop(0, levels, narrow, 0)
        for k, (low, high) in enumerate(cuts):
            if (high <= levels) == (part == 0):
                send(backbuf, backrecv, low, high - low, back_send_sem, back_recv_sem.at[k])
        placed.start()

    def unpack(first, count, slot):
        for d in range(n):
            for i in range(own):
                rows = backrecv[d, pl.ds(first, count), lats * i : lats * (i + 1)]
                turned_back[own * d + i, :count] = rows.astype(jnp.float32)
        for c in range(count):
            flat = jnp.where(live[...] > 0.5, turned_back[:, c, :].T, 0.0)
            outbuf[slot, c] = flat.astype(jnp.bfloat16)

    def put(first, count, slot):
        return pltpu.make_async_copy(
            outbuf.at[slot, pl.ds(0, count)], rows_out.at[pl.ds(first, count)], out_sem.at[slot]
        )

    def unpack_step(g, carry):
        slot = lax.rem(g, 2)
        for k, (low, high) in enumerate(cuts):

            @pl.when(g == low // STEP)
            def _():
                landed = backrecv.at[:, pl.ds(low, high - low)]
                pltpu.make_async_copy(landed, landed, back_recv_sem.at[k]).wait()

        @pl.when(g >= 2)
        def _():
            put((g - 2) * STEP, STEP, slot).wait()

        unpack(pl.multiple_of(g * STEP, STEP), STEP, slot)
        put(g * STEP, STEP, slot).start()
        return carry

    lax.fori_loop(0, full, unpack_step, 0)
    ends = [(g * STEP, STEP, g % 2) for g in (full - 2, full - 1)]
    if tail:
        put(*ends.pop(0)).wait()
        ends.append((full * STEP, tail, full % 2))
        unpack(*ends[-1])
        put(*ends[-1]).start()
    for end in ends:
        put(*end).wait()
    placed.wait()
    sent = sendbuf.at[pl.ds(0, n - 1)]
    pltpu.make_async_copy(sent, sent, send_sem).wait()
    sent = backbuf.at[pl.ds(0, n - 1)]
    pltpu.make_async_copy(sent, sent, back_send_sem).wait()


def per_device(
    n, north_rows, south_rows, lon_counts, slot_wave, legendre, mode_rates, to_modes, from_modes
):
    lats = north_rows.shape[0]
    own, row_total, lat_total = legendre.shape
    levels = to_modes.shape[0]
    slots = slot_wave.shape[0]
    total = 2 * levels
    north = jnp.transpose(north_rows, (2, 0, 1))
    south = jnp.transpose(south_rows, (2, 0, 1))
    smem = pl.BlockSpec(memory_space=pltpu.SMEM)
    vmem = pl.BlockSpec(memory_space=pltpu.VMEM)
    hbm = pl.BlockSpec(memory_space=pl.ANY)
    bf16, f32 = jnp.bfloat16, jnp.float32
    dma = pltpu.SemaphoreType.DMA
    width = own * lats
    spec, rows = pl.pallas_call(
        functools.partial(step_kernel, n, own, lats, levels),
        in_specs=[smem, smem, vmem, vmem, vmem, vmem, hbm, hbm, hbm],
        out_specs=[hbm, hbm],
        out_shape=[
            jax.ShapeDtypeStruct((total, own, row_total), bf16),
            jax.ShapeDtypeStruct((total, lats, slots), bf16),
        ],
        scratch_shapes=[
            pltpu.VMEM((2, 2, STEP, lats, slots), bf16),
            pltpu.VMEM((lats, slots), f32),
            pltpu.VMEM((STEP, slots, lats), f32),
            pltpu.VMEM((n, total, width), bf16),
            pltpu.VMEM((n, total, width), bf16),
            pltpu.VMEM((own, levels, lat_total), bf16),
            pltpu.VMEM((own, levels, lat_total), bf16),
            pltpu.VMEM((2, row_total, lat_total), bf16),
            pltpu.VMEM((levels, levels), bf16),
            pltpu.VMEM((levels, levels), bf16),
            pltpu.VMEM((levels, 1), f32),
            pltpu.VMEM((levels, own, row_total), f32),
            pltpu.VMEM((levels, own, row_total), bf16),
            pltpu.VMEM((n, total, width), bf16),
            pltpu.VMEM((n, total, width), bf16),
            pltpu.VMEM((slots, STEP, lats), f32),
            pltpu.VMEM((2, STEP, lats, slots), bf16),
            dma((2, 2)),
            dma((2,)),
            dma,
            dma((2,)),
            dma,
            dma((len(back_cuts(levels)),)),
            dma,
            dma((2,)),
        ],
        compiler_params=pltpu.CompilerParams(
            vmem_limit_bytes=VMEM_LIMIT, collective_id=0, has_side_effects=True
        ),
        name="spectral_step",
    )(
        slot_wave, lon_counts, slot_wave[None, :], mode_rates[None, :], to_modes, from_modes,
        north, south, legendre,
    )
    return jnp.transpose(spec, (1, 2, 0)), jnp.transpose(rows, (1, 2, 0))


def solution(mesh):
    in_specs = (
        P(("grp", "wave"), None, None),
        P(("grp", "wave"), None, None),
        P(),
        P(),
        P("wave", None, None),
        P(),
        P(),
        P(),
    )
    out_specs = (P(("grp", "wave"), None, None), P(("grp", "wave"), None, None))
    body = functools.partial(per_device, mesh.shape["wave"])
    return jax.shard_map(
        body, mesh=mesh, in_specs=in_specs, out_specs=out_specs, check_vma=False
    )
```

time: 306 us -> 267 us (0.87)
  waiting for transfers between devices: 167 us -> 0 us
  Pallas kernels: 105 us -> 258 us
  starting transfers between devices: 20.8 us -> 0 us
  other arithmetic: 3.53 us -> 0 us
    all_to_all x4 -> x0, waiting for transfers between devices: 167 us -> none  [the longest x2 85.3 us: per_device(): home = lax.all_to_all(back, 'wave', split_axis=0, concat_axis=0, tiled=True)]
    pallas_call x6 -> x1, Pallas kernels: 105 us -> 258 us  [per_device(): pl.pallas_call(functools.partial(step_kernel, n, own, lats, levels), in_s...]
    all_to_all x4 -> x0, starting transfers between devices: 20.8 us -> none  [the longest x2 11.3 us: per_device(): lax.all_to_all(packed, 'wave', split_axis=0, concat_axis=0, tiled=True)]
    transpose x1 -> x0, other arithmetic: 3.53 us -> none  [per_device(): spec_state = jnp.transpose(jnp.concatenate(states, axis=0), (1, 2, 0))]
    unnamed x17 -> x4, local copies, waits for them, and re-layouts: 5.04 us -> 8.07 us
  transfers between devices with their start and end apart: 4 -> 0, of which waited for: 4 -> 0; matrix products, arithmetic and copies ran while one was open for 3% -> 0% of each run, Pallas kernels for 27% -> 0%
where the time goes in v1:
time: 267 us; the launch traced here: 266 us
  Pallas kernels  258 us (97%)
  local copies, waits for them, and re-layouts  8.07 us (3%)
    pallas_call x1, Pallas kernels, per_device(): pl.pallas_call(functools.partial(step_kernel, n, own, lats, levels), in_s...  258 us
    unnamed x4, local copies, waits for them, and re-layouts  8.07 us

profile of v1, /device:TPU:13, one launch (start us, length us, event | category | flops | bytes accessed | tf_op | source)
XLA Modules:
  0.0 266.3 jit_solution(10190346307756460591)
XLA Ops:
  0.6 257.6 %spectral_step.1 = (bf16[274,8,1280]{2,1,0:T(8,128)(2,1)}, bf16[274,80,128]{2,1,0:T(8,128)(2,1)}) custom-call(s32[128]{0:T(128)} %waves_s.1, s32[1280]{0:T(1024)} %counts_s.1, s32[1,128]{1,0:T(1,128)} %bitcast.10, f32[1,137]{1,0:T(1,128)} %bitcast.11, bf16[137,137]{1,0:T(8,128)(2,1)} %to_ref.1, bf16[137,137]{1,0:T(8,128)(2,1)} %from_ref.1, ...), custom_call_target="tpu_custom_call" | custom-call | tf_op jit(solution)/shard_map/spectral_step/pallas_call | solution.py:271
  258.2 0.0 copy-start
  258.2 5.6 %copy.12 = bf16[8,1280,274]{1,0,2:T(8,128)(2,1)} copy(bf16[8,1280,274]{1,0,2:T(8,128)(2,1)} %bitcast.9) | data formatting | bytes 11223040
  263.8 0.0 copy-done
  263.8 2.5 copy.13
Async XLA Ops:
  258.2 5.6 %copy-start = (bf16[274,80,128]{2,1,0:T(8,128)(2,1)S(1)}, bf16[274,80,128]{2,1,0:T(8,128)(2,1)}, u32[]{:S(2)}) copy-start(bf16[274,80,128]{2,1,0:T(8,128)(2,1)} %get-tuple-element.5) | copy-start | bytes 16834564

commit v2 on v1

--- a/solution.py
+++ b/solution.py
@@ -8,7 +8,7 @@
 from jax.sharding import PartitionSpec as P
 
 NMAX = 2559
-VMEM_LIMIT = 63 * 1024 * 1024
+VMEM_LIMIT = 50 * 1024 * 1024
 STEP = 16
 MESH = pl.DeviceIdType.MESH
 
@@ -34,9 +34,9 @@
     n, own, lats, levels,
     waves_s, counts_s, waves_ref, rates_ref, to_ref, from_ref, north, south, leg,
     spec_out, rows_out,
-    inbuf, live, turned, sendbuf, recv, columns, returned, legbuf, to_t, from_t, rates_col,
-    state_t, state_b, backbuf, backrecv, turned_back, outbuf,
-    in_sem, leg_sem, send_sem, recv_sem, back_send_sem, back_recv_sem, state_sem, out_sem,
+    inbuf, live, turned, sendbuf, recv, columns, legbuf, to_t, from_t, rates_col,
+    state_t, backbuf, backrecv, turned_back,
+    in_sem, leg_sem, send_sem, recv_sem, back_send_sem, back_recv_sem,
 ):
     me = lax.axis_index("wave")
     total = 2 * levels
@@ -176,7 +176,7 @@
             state = jnp.where(degree <= NMAX, state, 0.0).astype(jnp.bfloat16)
             state_t[:, slot, :] = state.astype(jnp.float32)
             back = jnp.dot(state, legbuf[place], preferred_element_type=jnp.float32)
-            returned[slot] = back.astype(jnp.bfloat16)
+            columns[slot] = back.astype(jnp.bfloat16)
             later = slot + 2
 
             @pl.when(own * part + later < 2 * own)
@@ -188,39 +188,29 @@
         lax.fori_loop(0, own, solve, 0)
         for s in range(own):
             for d in range(n):
-                backbuf[d, base : base + levels, lats * s : lats * (s + 1)] = returned[
+                backbuf[d, base : base + levels, lats * s : lats * (s + 1)] = columns[
                     s, :, lats * d : lats * (d + 1)
                 ]
-        placed = pltpu.make_async_copy(state_b, spec_out.at[pl.ds(base, levels)], state_sem)
-        if part == 1:
-            pltpu.make_async_copy(state_b, spec_out.at[pl.ds(0, levels)], state_sem).wait()
 
         def narrow(l, carry):
-            state_b[l] = state_t[l].astype(jnp.bfloat16)
+            spec_out[base + l] = state_t[l].astype(jnp.bfloat16)
             return carry
 
         lax.fori_loop(0, levels, narrow, 0)
         for k, (low, high) in enumerate(cuts):
             if (high <= levels) == (part == 0):
                 send(backbuf, backrecv, low, high - low, back_send_sem, back_recv_sem.at[k])
-        placed.start()
-
-    def unpack(first, count, slot):
+
+    def unpack(first, count):
         for d in range(n):
             for i in range(own):
                 rows = backrecv[d, pl.ds(first, count), lats * i : lats * (i + 1)]
                 turned_back[own * d + i, :count] = rows.astype(jnp.float32)
         for c in range(count):
             flat = jnp.where(live[...] > 0.5, turned_back[:, c, :].T, 0.0)
-            outbuf[slot, c] = flat.astype(jnp.bfloat16)
-
-    def put(first, count, slot):
-        return pltpu.make_async_copy(
-            outbuf.at[slot, pl.ds(0, count)], rows_out.at[pl.ds(first, count)], out_sem.at[slot]
-        )
+            rows_out[first + c] = flat.astype(jnp.bfloat16)
 
     def unpack_step(g, carry):
-        slot = lax.rem(g, 2)
         for k, (low, high) in enumerate(cuts):
 
             @pl.when(g == low // STEP)
@@ -228,24 +218,12 @@
                 landed = backrecv.at[:, pl.ds(low, high - low)]
                 pltpu.make_async_copy(landed, landed, back_recv_sem.at[k]).wait()
 
-        @pl.when(g >= 2)
-        def _():
-            put((g - 2) * STEP, STEP, slot).wait()
-
-        unpack(pl.multiple_of(g * STEP, STEP), STEP, slot)
-        put(g * STEP, STEP, slot).start()
+        unpack(pl.multiple_of(g * STEP, STEP), STEP)
         return carry
 
     lax.fori_loop(0, full, unpack_step, 0)
-    ends = [(g * STEP, STEP, g % 2) for g in (full - 2, full - 1)]
     if tail:
-        put(*ends.pop(0)).wait()
-        ends.append((full * STEP, tail, full % 2))
-        unpack(*ends[-1])
-        put(*ends[-1]).start()
-    for end in ends:
-        put(*end).wait()
-    placed.wait()
+        unpack(full * STEP, tail)
     sent = sendbuf.at[pl.ds(0, n - 1)]
     pltpu.make_async_copy(sent, sent, send_sem).wait()
     sent = backbuf.at[pl.ds(0, n - 1)]
@@ -271,10 +249,10 @@
     spec, rows = pl.pallas_call(
         functools.partial(step_kernel, n, own, lats, levels),
         in_specs=[smem, smem, vmem, vmem, vmem, vmem, hbm, hbm, hbm],
-        out_specs=[hbm, hbm],
+        out_specs=[vmem, vmem],
         out_shape=[
-            jax.ShapeDtypeStruct((total, own, row_total), bf16),
-            jax.ShapeDtypeStruct((total, lats, slots), bf16),
+            pltpu.VMEM((total, own, row_total), bf16),
+            pltpu.VMEM((total, lats, slots), bf16),
         ],
         scratch_shapes=[
             pltpu.VMEM((2, 2, STEP, lats, slots), bf16),
@@ -283,25 +261,20 @@
             pltpu.VMEM((n, total, width), bf16),
             pltpu.VMEM((n, total, width), bf16),
             pltpu.VMEM((own, levels, lat_total), bf16),
-            pltpu.VMEM((own, levels, lat_total), bf16),
             pltpu.VMEM((2, row_total, lat_total), bf16),
             pltpu.VMEM((levels, levels), bf16),
             pltpu.VMEM((levels, levels), bf16),
             pltpu.VMEM((levels, 1), f32),
             pltpu.VMEM((levels, own, row_total), f32),
-            pltpu.VMEM((levels, own, row_total), bf16),
             pltpu.VMEM((n, total, width), bf16),
             pltpu.VMEM((n, total, width), bf16),
             pltpu.VMEM((slots, STEP, lats), f32),
-            pltpu.VMEM((2, STEP, lats, slots), bf16),
             dma((2, 2)),
             dma((2,)),
             dma,
             dma((2,)),
             dma,
             dma((len(back_cuts(levels)),)),
-            dma,
-            dma((2,)),
         ],
         compiler_params=pltpu.CompilerParams(
             vmem_limit_bytes=VMEM_LIMIT, collective_id=0, has_side_effects=True

time: 267 us -> 262 us (0.981)
  local copies, waits for them, and re-layouts: 8.07 us -> 4.96 us
    unnamed x4 -> x2, local copies, waits for them, and re-layouts: 8.07 us -> 4.96 us
where the time goes in v2:
time: 262 us
  Pallas kernels  256 us (98%)
  local copies, waits for them, and re-layouts  4.96 us (2%)
    pallas_call x1, Pallas kernels, per_device(): pl.pallas_call(functools.partial(step_kernel, n, own, lats, levels), in_s...  256 us

profile of v2, /device:TPU:13, one launch (start us, length us, event | category | flops | bytes accessed | tf_op | source)
XLA Modules:
  0.0 262.1 jit_solution(17361318091491657262)
XLA Ops:
  0.6 256.5 %spectral_step.1 = (bf16[274,8,1280]{2,1,0:T(8,128)(2,1)S(1)}, bf16[274,80,128]{2,1,0:T(8,128)(2,1)S(1)}) custom-call(s32[128]{0:T(128)} %waves_s.1, s32[1280]{0:T(1024)} %counts_s.1, s32[1,128]{1,0:T(1,128)} %bitcast.10, f32[1,137]{1,0:T(1,128)} %bitcast.11, bf16[137,137]{1,0:T(8,128)(2,1)} %to_ref.1, bf16[137,137]{1,0:T(8,128)(2,1)} %from_ref.1, ...), custom_call_target="tpu_custom_call" | custom-call | tf_op jit(solution)/shard_map/spectral_step/pallas_call | solution.py:249
  257.1 2.5 copy.12
  259.6 2.5 copy.13

commit v3 on v2

--- a/solution.py
+++ b/solution.py
@@ -26,8 +26,12 @@
     for part in (1, 2):
         cuts.append(ready + rest * part // 3 * STEP)
     cuts.append(total // STEP * STEP - STEP)
-    cuts.append(total)
+    cuts.append(total // STEP * STEP)
     return tuple(zip(cuts[:-1], cuts[1:]))
+
+
+def tail_rows(total, width):
+    return max(align(total % STEP * pl.cdiv(width, 128)), STEP)
 
 
 def step_kernel(
@@ -35,8 +39,9 @@
     waves_s, counts_s, waves_ref, rates_ref, to_ref, from_ref, north, south, leg,
     spec_out, rows_out,
     inbuf, live, turned, sendbuf, recv, columns, legbuf, to_t, from_t, rates_col,
-    state_t, backbuf, backrecv, turned_back,
+    state_t, backbuf, backrecv, turned_back, tail_out, tail_in, tail_back, tail_home,
     in_sem, leg_sem, send_sem, recv_sem, back_send_sem, back_recv_sem,
+    tail_send_sem, tail_recv_sem,
 ):
     me = lax.axis_index("wave")
     total = 2 * levels
@@ -78,6 +83,9 @@
         return carry
 
     lax.fori_loop(0, lats, fill, 0)
+    tail_out[...] = jnp.zeros_like(tail_out)
+    tail_back[...] = jnp.zeros_like(tail_back)
+    packed_rows = tail_out.shape[1]
 
     def send(src, dst, first, count, ssem, rsem):
         rows = pl.ds(first, count)
@@ -97,6 +105,28 @@
         lax.fori_loop(1, n, one, 0)
         pltpu.make_async_copy(src.at[me, rows], dst.at[me, rows], rsem).start()
 
+    def narrow_tail(buf, packed):
+        def one(d, carry):
+            for t in range(pl.cdiv(own * lats, 128)):
+                lanes = slice(128 * t, min(128 * (t + 1), own * lats))
+                place = slice(tail * t, tail * (t + 1))
+                packed[d, place, : lanes.stop - lanes.start] = buf[d, full * STEP : total, lanes]
+            return carry
+
+        lax.fori_loop(0, n, one, 0)
+
+    def widen_tail(packed, buf, rsem):
+        pltpu.make_async_copy(packed, packed, rsem).wait()
+
+        def one(d, carry):
+            for t in range(pl.cdiv(own * lats, 128)):
+                lanes = slice(128 * t, min(128 * (t + 1), own * lats))
+                place = slice(tail * t, tail * (t + 1))
+                buf[d, full * STEP : total, lanes] = packed[d, place, : lanes.stop - lanes.start]
+            return carry
+
+        lax.fori_loop(0, n, one, 0)
+
     def pack(first, count, slot):
         sums = inbuf[slot, 0, :count].astype(jnp.float32) + inbuf[slot, 1, :count].astype(jnp.float32)
         kept = jnp.where(live[...][None] > 0.5, sums, 0.0).astype(jnp.bfloat16)
@@ -139,6 +169,7 @@
         for copy in fetch(full * STEP, tail, 0):
             copy.wait()
         pack(full * STEP, tail, 0)
+        narrow_tail(sendbuf, tail_out)
     for slot in range(2):
         fetch_leg(slot, slot).start()
     to_t[...] = to_ref[...].astype(jnp.float32).T.astype(jnp.bfloat16)
@@ -147,11 +178,23 @@
     down = lax.broadcasted_iota(jnp.int32, (levels, levels), 0)
     spread = jnp.where(across == down, jnp.broadcast_to(rates_ref[...], (levels, levels)), 0.0)
     rates_col[...] = jnp.sum(spread, axis=1, keepdims=True)
-    send(sendbuf, recv, last, STEP + tail, send_sem, recv_sem.at[1])
+    send(sendbuf, recv, last, STEP, send_sem, recv_sem.at[1])
+    if tail:
+        send(tail_out, tail_in, 0, packed_rows, tail_send_sem.at[0], tail_recv_sem.at[0])
+
+    def send_piece(low, high, k):
+        def one_step(g, carry):
+            first = pl.multiple_of(low + g * STEP, STEP)
+            send(backbuf, backrecv, first, STEP, back_send_sem, back_recv_sem.at[k])
+            return carry
+
+        lax.fori_loop(0, (high - low) // STEP, one_step, 0)
 
     for part in range(2):
-        arrived = recv.at[:, pl.ds(split * part, (split, total - split)[part])]
+        arrived = recv.at[:, pl.ds(split * part, (split, full * STEP - split)[part])]
         pltpu.make_async_copy(arrived, arrived, recv_sem.at[part]).wait()
+        if tail and part == 1:
+            widen_tail(tail_in, recv, tail_recv_sem.at[0])
         base = levels * part
         for s in range(own):
             for d in range(n):
@@ -192,6 +235,9 @@
                     s, :, lats * d : lats * (d + 1)
                 ]
 
+        if tail and part == 1:
+            narrow_tail(backbuf, tail_back)
+
         def narrow(l, carry):
             spec_out[base + l] = state_t[l].astype(jnp.bfloat16)
             return carry
@@ -199,7 +245,9 @@
         lax.fori_loop(0, levels, narrow, 0)
         for k, (low, high) in enumerate(cuts):
             if (high <= levels) == (part == 0):
-                send(backbuf, backrecv, low, high - low, back_send_sem, back_recv_sem.at[k])
+                send_piece(low, high, k)
+        if tail and part == 1:
+            send(tail_back, tail_home, 0, packed_rows, tail_send_sem.at[1], tail_recv_sem.at[1])
 
     def unpack(first, count):
         for d in range(n):
@@ -223,10 +271,14 @@
 
     lax.fori_loop(0, full, unpack_step, 0)
     if tail:
+        widen_tail(tail_home, backrecv, tail_recv_sem.at[1])
         unpack(full * STEP, tail)
-    sent = sendbuf.at[pl.ds(0, n - 1)]
+        for k, buf in enumerate((tail_out, tail_back)):
+            sent = buf.at[pl.ds(0, n - 1)]
+            pltpu.make_async_copy(sent, sent, tail_send_sem.at[k]).wait()
+    sent = sendbuf.at[pl.ds(0, n - 1), pl.ds(0, full * STEP)]
     pltpu.make_async_copy(sent, sent, send_sem).wait()
-    sent = backbuf.at[pl.ds(0, n - 1)]
+    sent = backbuf.at[pl.ds(0, n - 1), pl.ds(0, full * STEP)]
     pltpu.make_async_copy(sent, sent, back_send_sem).wait()
 
 
@@ -269,12 +321,15 @@
             pltpu.VMEM((n, total, width), bf16),
             pltpu.VMEM((n, total, width), bf16),
             pltpu.VMEM((slots, STEP, lats), f32),
+            *[pltpu.VMEM((n, tail_rows(total, width), 128), bf16)] * 4,
             dma((2, 2)),
             dma((2,)),
             dma,
             dma((2,)),
             dma,
             dma((len(back_cuts(levels)),)),
+            dma((2,)),
+            dma((2,)),
         ],
         compiler_params=pltpu.CompilerParams(
             vmem_limit_bytes=VMEM_LIMIT, collective_id=0, has_side_effects=True

time: 262 us -> 258 us (0.985)
  Pallas kernels: 256 us -> 251 us
    pallas_call x1, Pallas kernels: 256 us -> 251 us  [per_device(): pl.pallas_call(functools.partial(step_kernel, n, own, lats, levels), in_s...]
where the time goes in v3:
time: 258 us; the launch traced here: 256 us
  Pallas kernels  251 us (97%)
  local copies, waits for them, and re-layouts  4.96 us (2%)
    pallas_call x1, Pallas kernels, per_device(): pl.pallas_call(functools.partial(step_kernel, n, own, lats, levels), in_s...  251 us

profile of v3, /device:TPU:13, one launch (start us, length us, event | category | flops | bytes accessed | tf_op | source)
XLA Modules:
  0.0 256.3 jit_solution(14156047488597714554)
XLA Ops:
  0.6 250.7 %spectral_step.1 = (bf16[274,8,1280]{2,1,0:T(8,128)(2,1)S(1)}, bf16[274,80,128]{2,1,0:T(8,128)(2,1)S(1)}) custom-call(s32[128]{0:T(128)} %waves_s.1, s32[1280]{0:T(1024)} %counts_s.1, s32[1,128]{1,0:T(1,128)} %bitcast.10, f32[1,137]{1,0:T(1,128)} %bitcast.11, bf16[137,137]{1,0:T(8,128)(2,1)} %to_ref.1, bf16[137,137]{1,0:T(8,128)(2,1)} %from_ref.1, ...), custom_call_target="tpu_custom_call" | custom-call | tf_op jit(solution)/shard_map/spectral_step/pallas_call | solution.py:301
  251.4 2.5 copy.12
  253.8 2.5 copy.13
